TPU v7x, 32 devices: a whole 2x2x4 slice. The times are simulated.
32 devices in a mesh: seq: 8 (over z, y), tok: 4 (over x, core).
Axes of the slice: x: 2, y: 2, z: 4, core: 2. Of those that a mesh axis runs over, the one named last changes fastest.
Arguments:
- tokens: bfloat16 [8, 1024, 1024], P('seq', 'tok'), may hold values from -6 to 6
- out_grad: bfloat16 [8, 1024, 1024], P('seq', 'tok'), may hold values from -6 to 6
- segments: int32 [8, 1024], P('seq'), may hold values from 0 to 2, never falling along the last dimension, each value on 1 to 512 neighbouring positions
- adapter_index: int32 [8], P('seq'), may hold values from 0 to 7
- qkv_weight: bfloat16 [1024, 3072], P('tok', 'seq'), may hold values from -0.1875 to 0.1875
- out_weight: bfloat16 [1024, 1024], P('tok', 'seq'), may hold values from -0.75 to 0.75
- in_weight: bfloat16 [1024, 5248], P('tok', 'seq'), may hold values from -0.1875 to 0.1875
- out2_weight: bfloat16 [2624, 1024], P('tok', 'seq'), may hold values from -0.15625 to 0.15625
- attn_gain: bfloat16 [1024], P('tok'), may hold values from 0.099609375 to 1.8984375
- mlp_gain: bfloat16 [1024], P('tok'), may hold values from 0.099609375 to 1.8984375
- qkv_down: bfloat16 [8, 16, 1024], replicated, may hold values from -0.1875 to 0.1875
- qkv_up: bfloat16 [8, 16, 3072], replicated, may hold values from -0.5 to 0.5
- out_down: bfloat16 [8, 16, 1024], replicated, may hold values from -0.1875 to 0.1875
- out_up: bfloat16 [8, 16, 1024], replicated, may hold values from -1.5 to 1.5
- in_down: bfloat16 [8, 16, 1024], replicated, may hold values from -0.1875 to 0.1875
- in_up: bfloat16 [8, 16, 5248], replicated, may hold values from -0.5 to 0.5
- out2_down: bfloat16 [8, 16, 2624], replicated, may hold values from -0.125 to 0.125
- out2_up: bfloat16 [8, 16, 1024], replicated, may hold values from -0.5 to 0.5
Outputs:
- layer_out: bfloat16 [8, 1024, 1024], P('seq', 'tok')
- input_grad: bfloat16 [8, 1024, 1024], P('seq', 'tok')
- qkv_down_grad: float32 [8, 16, 1024], replicated
- qkv_up_grad: float32 [8, 16, 3072], replicated
- out_down_grad: float32 [8, 16, 1024], replicated
- out_up_grad: float32 [8, 16, 1024], replicated
- in_down_grad: float32 [8, 16, 1024], replicated
- in_up_grad: float32 [8, 16, 5248], replicated
- out2_down_grad: float32 [8, 16, 2624], replicated
- out2_up_grad: float32 [8, 16, 1024], replicated
Inputs may be any that keep to these rules, and one draw needn't show every extreme that they name: `segments`: within a sequence the document numbers never fall; each document has 1 to 512 tokens, one of each sequence exactly 512.
All inputs are finite; a program needn't handle non-finite values.
Results may differ from a plain program's by a relative error of at most 0.018.
Values may be sent and summed in bfloat16 or wider, within the bound.
No kernel may reach another device: no remote copies, remote signals or barrier semaphores. Data moves between devices by JAX's collectives and lax.ppermute only.
A program may use at most 128 MiB of HBM per device.

v0:
```python
import jax
import jax.numpy as jnp
from jax import lax
from jax.sharding import PartitionSpec as P

HEADS = 16
HEAD_DIM = 64
FF = 2624
ADAPTERS = 8
EPS = 1e-05
THETA = 160000.0
HIGH = lax.Precision.HIGHEST


def layer_norm(values, gain_vec):
    middle = jnp.mean(values, axis=-1, keepdims=True)
    centered = values - middle
    spread = jnp.mean(centered * centered, axis=-1, keepdims=True)
    return centered * lax.rsqrt(spread + EPS) * gain_vec


def rotary_table(positions, head_width):
    exponent = jnp.arange(0, head_width, 2).astype(jnp.float32) / head_width
    inverse = 1.0 / THETA**exponent
    phases = positions.astype(jnp.float32)[:, None] * inverse[None, :]
    cosine = jnp.concatenate([jnp.cos(phases), jnp.cos(phases)], -1)
    sine_part = jnp.concatenate([jnp.sin(phases), jnp.sin(phases)], -1)
    return (cosine, sine_part)


def rotary(values, cosine, sine_part):
    half_width = values.shape[-1] // 2
    turned = jnp.concatenate([-values[..., half_width:], values[..., :half_width]], -1)
    return values * cosine[None, :, None, :] + turned * sine_part[None, :, None, :]


def glu_act(inputs, gate_vals):
    return jax.nn.gelu(inputs, approximate=False) * gate_vals


def select(table_rows, onehot_low):
    return jnp.einsum(
        "sa,ayz->syz", onehot_low, table_rows, preferred_element_type=jnp.float32
    ).astype(jnp.bfloat16)


def spread_back(term_rows, onehot):
    return jnp.einsum(
        "sa,syz->ayz", onehot, term_rows, precision=HIGH, preferred_element_type=jnp.float32
    )


def project(inputs, weight, down_rows, up_rows):
    seq_count, row_count, width_in = inputs.shape
    main_part = jnp.dot(
        inputs.reshape(seq_count * row_count, width_in), weight, preferred_element_type=jnp.float32
    )
    narrow = jnp.einsum(
        "std,srd->str", inputs, down_rows, preferred_element_type=jnp.float32
    ).astype(jnp.bfloat16)
    extra_part = jnp.einsum("str,sre->ste", narrow, up_rows, preferred_element_type=jnp.float32)
    return (main_part.reshape(seq_count, row_count, -1) + extra_part, narrow)


def project_back(grad_out, inputs, narrow, weight, down_rows, up_rows):
    seq_count, row_count, width_out = grad_out.shape
    main_part = lax.dot_general(
        grad_out.reshape(seq_count * row_count, width_out),
        weight,
        (((1,), (1,)), ((), ())),
        preferred_element_type=jnp.float32,
    )
    inner_grad = jnp.einsum(
        "ste,sre->str", grad_out, up_rows, preferred_element_type=jnp.float32
    ).astype(jnp.bfloat16)
    back_sum = main_part.reshape(seq_count, row_count, -1) + jnp.einsum(
        "str,srd->std", inner_grad, down_rows, preferred_element_type=jnp.float32
    )
    grad_up = jnp.einsum("str,ste->sre", narrow, grad_out, preferred_element_type=jnp.float32)
    grad_down = jnp.einsum("str,std->srd", inner_grad, inputs, preferred_element_type=jnp.float32)
    return (back_sum, grad_down, grad_up)


def masked_scores(query_part, key_part, doc_mask):
    scores = (
        jnp.einsum("sqhd,skhd->shqk", query_part, key_part, preferred_element_type=jnp.float32)
        * 0.125
    )
    return jnp.where(doc_mask[:, None, :, :], scores, -1e30)


def heads_slice(source, group_index, group_width, head_width):
    part_cols = lax.dynamic_slice_in_dim(source, group_index * group_width, group_width, 2)
    return part_cols.reshape(
        part_cols.shape[0], part_cols.shape[1], group_width // head_width, head_width
    )


def join_groups(parts):
    moved = jnp.moveaxis(parts, 0, 2)
    return moved.reshape(moved.shape[0], moved.shape[1], -1)


def body(
    tokens,
    out_grad,
    segments,
    adapter_index,
    qkv_weight,
    out_weight,
    in_weight,
    out2_weight,
    attn_gain,
    mlp_gain,
    qkv_down,
    qkv_up,
    out_down,
    out_up,
    in_down,
    in_up,
    out2_down,
    out2_up,
):
    seq_count, tok_rows, model_width = tokens.shape
    head_width = HEAD_DIM
    group_width = 2 * head_width
    groups = jnp.arange(HEADS // 2)
    seq_length = segments.shape[1]
    tok_start = lax.axis_index("tok") * tok_rows
    positions = tok_start + jnp.arange(tok_rows)
    cosine, sine_part = rotary_table(positions, head_width)
    own_segments = lax.dynamic_slice_in_dim(segments, tok_start, tok_rows, 1)
    doc_mask = own_segments[:, :, None] == segments[:, None, :]
    pick_bits = adapter_index[:, None] == jnp.arange(ADAPTERS)[None, :]
    onehot = pick_bits.astype(jnp.float32)
    onehot_low = pick_bits.astype(jnp.bfloat16)
    picked = [
        select(table_rows, onehot_low)
        for table_rows in (qkv_down, qkv_up, out_down, out_up, in_down, in_up, out2_down, out2_up)
    ]
    tok_parts = (
        lax.all_gather(qkv_weight, "tok", axis=0, tiled=True),
        lax.all_gather(out_weight, "tok", axis=0, tiled=True),
        lax.all_gather(in_weight, "tok", axis=0, tiled=True),
        lax.all_gather(out2_weight, "tok", axis=0, tiled=True),
        lax.all_gather(attn_gain, "tok", axis=0, tiled=True),
        lax.all_gather(mlp_gain, "tok", axis=0, tiled=True),
    )
    w_qkv, w_out, w_in, w_out2 = (
        lax.all_gather(tok_parts[0], "seq", axis=1, tiled=True),
        lax.all_gather(tok_parts[1], "seq", axis=1, tiled=True),
        lax.all_gather(tok_parts[2], "seq", axis=1, tiled=True),
        lax.all_gather(tok_parts[3], "seq", axis=1, tiled=True),
    )
    gain_one = tok_parts[4].astype(jnp.float32)
    gain_two = tok_parts[5].astype(jnp.float32)
    inputs = tokens.astype(jnp.float32)
    norm_one = layer_norm(inputs, gain_one).astype(jnp.bfloat16)
    qkv, narrow_qkv = project(norm_one, w_qkv, picked[0], picked[1])
    head_shape = (seq_count, tok_rows, HEADS, head_width)
    query_pre = qkv[..., :model_width].reshape(head_shape)
    query_low = (
        rotary(query_pre, cosine, sine_part)
        .reshape(seq_count, tok_rows, model_width)
        .astype(jnp.bfloat16)
    )
    key_low = (
        rotary(qkv[..., model_width : 2 * model_width].reshape(head_shape), cosine, sine_part)
        .reshape(seq_count, tok_rows, model_width)
        .astype(jnp.bfloat16)
    )
    value_low = qkv[..., 2 * model_width :].astype(jnp.bfloat16)
    keys_all, values_all = (
        lax.all_gather(key_low, "tok", axis=1, tiled=True),
        lax.all_gather(value_low, "tok", axis=1, tiled=True),
    )

    def forward_group(group_index):
        query_part = heads_slice(query_low, group_index, group_width, head_width)
        key_part = heads_slice(keys_all, group_index, group_width, head_width)
        value_part = heads_slice(values_all, group_index, group_width, head_width)
        scores = masked_scores(query_part, key_part, doc_mask)
        row_max = jnp.max(scores, axis=-1, keepdims=True)
        row_total = jnp.sum(jnp.exp(scores - row_max), axis=-1, keepdims=True)
        log_total = row_max + jnp.log(row_total)
        attn_prob = jnp.exp(scores - log_total).astype(jnp.bfloat16)
        mixed = jnp.einsum(
            "shqk,skhd->sqhd", attn_prob, value_part, preferred_element_type=jnp.float32
        )
        return (mixed.reshape(seq_count, tok_rows, group_width), log_total[..., 0])

    mixed_parts, log_totals = lax.map(forward_group, groups)
    attn_low = join_groups(mixed_parts).astype(jnp.bfloat16)
    attn_branch, narrow_out = project(attn_low, w_out, picked[2], picked[3])
    middle = inputs + attn_branch
    norm_two = layer_norm(middle, gain_two).astype(jnp.bfloat16)
    gate_up, narrow_in = project(norm_two, w_in, picked[4], picked[5])
    act_low = glu_act(gate_up[..., :FF], gate_up[..., FF:]).astype(jnp.bfloat16)
    mlp_branch, narrow_out2 = project(act_low, w_out2, picked[6], picked[7])
    layer_out = (middle + mlp_branch).astype(jnp.bfloat16)
    back_parts = (
        lax.all_gather(qkv_weight, "tok", axis=0, tiled=True),
        lax.all_gather(out_weight, "tok", axis=0, tiled=True),
        lax.all_gather(in_weight, "tok", axis=0, tiled=True),
        lax.all_gather(out2_weight, "tok", axis=0, tiled=True),
    )
    w_qkv, w_out, w_in, w_out2 = (
        lax.all_gather(back_parts[0], "seq", axis=1, tiled=True),
        lax.all_gather(back_parts[1], "seq", axis=1, tiled=True),
        lax.all_gather(back_parts[2], "seq", axis=1, tiled=True),
        lax.all_gather(back_parts[3], "seq", axis=1, tiled=True),
    )
    grad_y = out_grad.astype(jnp.float32)
    back_act, down_o2, up_o2 = project_back(
        out_grad, act_low, narrow_out2, w_out2, picked[6], picked[7]
    )
    _, glu_back = jax.vjp(glu_act, gate_up[..., :FF], gate_up[..., FF:])
    grad_in, grad_gate = glu_back(back_act)
    grad_z = jnp.concatenate([grad_in, grad_gate], axis=-1).astype(jnp.bfloat16)
    back_norm_two, down_in, up_in = project_back(
        grad_z, norm_two, narrow_in, w_in, picked[4], picked[5]
    )
    _, norm_two_back = jax.vjp(lambda field: layer_norm(field, gain_two), middle)
    grad_mid = grad_y + norm_two_back(back_norm_two)[0]
    grad_a = grad_mid.astype(jnp.bfloat16)
    back_attn, down_out, up_out = project_back(
        grad_a, attn_low, narrow_out, w_out, picked[2], picked[3]
    )
    grad_attn = back_attn.astype(jnp.bfloat16)

    def query_grads(group_index):
        query_part = heads_slice(query_low, group_index, group_width, head_width)
        key_part = heads_slice(keys_all, group_index, group_width, head_width)
        value_part = heads_slice(values_all, group_index, group_width, head_width)
        grad_part = heads_slice(grad_attn, group_index, group_width, head_width)
        scores = masked_scores(query_part, key_part, doc_mask)
        attn_prob = jnp.exp(scores - log_totals[group_index][..., None])
        grad_prob = jnp.einsum(
            "sqhd,skhd->shqk", grad_part, value_part, preferred_element_type=jnp.float32
        )
        row_dot = jnp.sum(attn_prob * grad_prob, axis=-1)
        grad_scores = (attn_prob * (grad_prob - row_dot[..., None]) * 0.125).astype(jnp.bfloat16)
        grad_query = jnp.einsum(
            "shqk,skhd->sqhd", grad_scores, key_part, preferred_element_type=jnp.float32
        )
        return (
            query_part,
            grad_part,
            attn_prob,
            grad_scores,
            grad_query.reshape(seq_count, tok_rows, group_width),
            row_dot,
        )

    def summed_group(group_index):
        query_part, grad_part, attn_prob, grad_scores, grad_query, row_dot = query_grads(
            group_index
        )
        grad_key = jnp.einsum(
            "shqk,sqhd->skhd", grad_scores, query_part, preferred_element_type=jnp.float32
        )
        grad_value = jnp.einsum(
            "shqk,sqhd->skhd",
            attn_prob.astype(jnp.bfloat16),
            grad_part,
            preferred_element_type=jnp.float32,
        )
        grad_key, grad_value = (
            lax.psum_scatter(
                grad_key.reshape(seq_count, seq_length, group_width).astype(jnp.bfloat16),
                "tok",
                scatter_dimension=1,
                tiled=True,
            ).astype(jnp.float32),
            lax.psum_scatter(
                grad_value.reshape(seq_count, seq_length, group_width).astype(jnp.bfloat16),
                "tok",
                scatter_dimension=1,
                tiled=True,
            ).astype(jnp.float32),
        )
        return (grad_query, grad_key, grad_value)

    query_parts, key_parts, value_parts = lax.map(summed_group, groups)
    grad_query = join_groups(query_parts)
    grad_key = join_groups(key_parts)
    grad_value = join_groups(value_parts)
    _, rotate_back = jax.vjp(lambda field: rotary(field, cosine, sine_part), query_pre)
    grad_query_pre = rotate_back(grad_query.reshape(head_shape))[0].reshape(
        seq_count, tok_rows, model_width
    )
    grad_key_pre = rotate_back(grad_key.reshape(head_shape))[0].reshape(
        seq_count, tok_rows, model_width
    )
    grad_qkv = jnp.concatenate([grad_query_pre, grad_key_pre, grad_value], axis=-1).astype(
        jnp.bfloat16
    )
    back_norm_one, down_qkv, up_qkv = project_back(
        grad_qkv, norm_one, narrow_qkv, w_qkv, picked[0], picked[1]
    )
    _, norm_one_back = jax.vjp(lambda field: layer_norm(field, gain_one), inputs)
    input_grad = (grad_mid + norm_one_back(back_norm_one)[0]).astype(jnp.bfloat16)
    terms = (down_qkv, up_qkv, down_out, up_out, down_in, up_in, down_o2, up_o2)
    summed = lax.psum(
        (
            spread_back(terms[0], onehot),
            spread_back(terms[1], onehot),
            spread_back(terms[2], onehot),
            spread_back(terms[3], onehot),
            spread_back(terms[4], onehot),
            spread_back(terms[5], onehot),
            spread_back(terms[6], onehot),
            spread_back(terms[7], onehot),
        ),
        ("seq", "tok"),
    )
    return (
        layer_out,
        input_grad,
        summed[0],
        summed[1],
        summed[2],
        summed[3],
        summed[4],
        summed[5],
        summed[6],
        summed[7],
    )


def solution(mesh):
    return jax.shard_map(
        body,
        mesh=mesh,
        in_specs=(
            P("seq", "tok", None),
            P("seq", "tok", None),
            P("seq", None),
            P("seq"),
            P("tok", "seq"),
            P("tok", "seq"),
            P("tok", "seq"),
            P("tok", "seq"),
            P("tok"),
            P("tok"),
            P(),
            P(),
            P(),
            P(),
            P(),
            P(),
            P(),
            P(),
        ),
        out_specs=(
            P("seq", "tok", None),
            P("seq", "tok", None),
            P(),
            P(),
            P(),
            P(),
            P(),
            P(),
            P(),
            P(),
        ),
        check_vma=False,
    )
```

profile of v0, /device:TPU:0, one launch (start us, length us, event | category | flops | bytes accessed | tf_op | source)
XLA Modules:
  0.0 1193.3 jit_solution(8519961414103918297)
XLA Ops:
  7.3 11.8 all_gather.45
  19.9 8.8 all_gather.54
  28.7 5.2 all-gather
  44.1 75.4 %all-gather.10.cloned.1.call-done = bf16[1024,3072]{1,0:T(8,128)(2,1)} async-done(((bf16[1024,384]{1,0:T(8,128)(2,1)}), bf16[1024,3072]{1,0:T(8,128)(2,1)}) %all-gather.10.cloned.1.call-update) | async-done | bytes 6291472 | tf_op jit(solution)/shard_map/all_gather | solution.py:150
  119.5 4.6 fusion.117
  142.6 4.2 add_convert_fusion.4
  149.3 6.4 all_gather.49
  156.6 5.5 all-gather.1
  169.6 59.1 %all-gather.22.cloned.1.call-done = bf16[2624,1024]{1,0:T(8,128)(2,1)} async-done(((bf16[2624,128]{1,0:T(8,128)(2,1)}), bf16[2624,1024]{1,0:T(8,128)(2,1)}) %all-gather.22.cloned.1.call-update) | async-done | bytes 5373968 | tf_op jit(solution)/shard_map/all_gather | solution.py:153
  228.7 4.2 fusion.71
  236.1 15.5 %all-gather.14.cloned.1.call-done = bf16[1,1024,1024]{2,1,0:T(8,128)(2,1)} async-done(((bf16[1,256,1024]{2,1,0:T(8,128)(2,1)}), bf16[1,1024,1024]{2,1,0:T(8,128)(2,1)}) %all-gather.14.cloned.1.call-update) | async-done | bytes 2097168 | tf_op jit(solution)/shard_map/all_gather | solution.py:174
  251.5 4.0 copy.83
  255.5 20.6 %all-gather.12.cloned.1.call-done = bf16[1,1024,1024]{2,1,0:T(8,128)(2,1)} async-done(((bf16[1,256,1024]{2,1,0:T(8,128)(2,1)}), bf16[1,1024,1024]{2,1,0:T(8,128)(2,1)}) %all-gather.12.cloned.1.call-update) | async-done | bytes 2097168 | tf_op jit(solution)/shard_map/all_gather | solution.py:175
  276.1 4.0 copy.81
  280.1 45.8 %while.30 = (s32[]{:T(128)}, bf16[8,1,256,128]{2,3,1,0:T(8,128)(2,1)S(1)}, f32[8,1,2,256]{3,2,1,0:T(2,128)}, s32[8]{0:T(128)S(1)}, bf16[1,1024,1024]{1,2,0:T(8,1...) while((s32[]{:T(128)}, ...), condition=%wide.region_5.6_spmd.clone.clone, body=%wide.region_2.5_spmd.clone.sunk.clone | while | flops 138149376 | bytes 8804011 | solution.py:192
  326.1 3.1 all-gather.16.cloned.1.call-done
  332.7 151.0 %all-gather.20.cloned.1.call-done = bf16[1024,5248]{0,1:T(8,128)(2,1)} async-done(((bf16[1024,656]{0,1:T(8,128)(2,1)}), bf16[1024,5248]{0,1:T(8,128)(2,1)}) %all-gather.20.cloned.1.call-update) | async-done | bytes 10747920 | tf_op jit(solution)/shard_map/all_gather | solution.py:152
  483.7 6.0 fusion.119
  491.5 6.7 fusion.48
  503.0 3.0 fusion.61
  511.9 468.5 %while.31 = (s32[]{:T(128)}, f32[8,1,256,128]{2,3,1,0:T(8,128)}, f32[8,1,256,128]{2,3,1,0:T(8,128)}, bf16[8,1,256,128]{2,3,1,0:T(8,128)(2,1)}, s32[8]{0:T(128)S(...) while((s32[]{:T(128)}, f32[8,1,256,128]{2,3,1,0:T(8,128)}, ...), condition=%wide.region_14.15_spmd.clone.clone, body=%wide.region_10.14_spmd.clone.sunk.clone | while | flops 343477248 | bytes 23342488 | solution.py:284
  522.8 3.6 fusion.229
  526.4 2.6 convolution_convert_fusion.11
  529.1 3.6 fusion.228
  534.2 10.5 reduce-scatter.3.cloned.1.call-done
  546.3 21.2 %reduce-scatter.5.cloned.1.call-done = bf16[1,256,128]{1,2,0:T(8,128)(2,1)} async-done(((bf16[1,1024,128]{1,2,0:T(8,128)(2,1)}), bf16[1,256,128]{1,2,0:T(8,128)(2,1)}) %reduce-scatter.5.cloned.1.call-update) | async-done | bytes 65552 | tf_op jit(solution)/shard_map/while/body/eval_jaxpr/reduce_scatter | solution.py:275
  579.8 3.6 fusion.229
  583.4 2.6 convolution_convert_fusion.11
  586.1 3.5 fusion.228
  591.2 12.4 %reduce-scatter.3.cloned.1.call-done = bf16[1,256,128]{1,2,0:T(8,128)(2,1)} async-done(((bf16[1,1024,128]{1,2,0:T(8,128)(2,1)}), bf16[1,256,128]{1,2,0:T(8,128)(2,1)}) %reduce-scatter.3.cloned.1.call-update) | async-done | bytes 65552 | tf_op jit(solution)/shard_map/while/body/eval_jaxpr/reduce_scatter | solution.py:269
  605.1 21.1 %reduce-scatter.5.cloned.1.call-done = bf16[1,256,128]{1,2,0:T(8,128)(2,1)} async-done(((bf16[1,1024,128]{1,2,0:T(8,128)(2,1)}), bf16[1,256,128]{1,2,0:T(8,128)(2,1)}) %reduce-scatter.5.cloned.1.call-update) | async-done | bytes 65552 | tf_op jit(solution)/shard_map/while/body/eval_jaxpr/reduce_scatter | solution.py:275
  638.6 3.6 fusion.229
  642.2 2.6 convolution_convert_fusion.11
  644.9 3.5 fusion.228
  650.0 12.4 %reduce-scatter.3.cloned.1.call-done = bf16[1,256,128]{1,2,0:T(8,128)(2,1)} async-done(((bf16[1,1024,128]{1,2,0:T(8,128)(2,1)}), bf16[1,256,128]{1,2,0:T(8,128)(2,1)}) %reduce-scatter.3.cloned.1.call-update) | async-done | bytes 65552 | tf_op jit(solution)/shard_map/while/body/eval_jaxpr/reduce_scatter | solution.py:269
  663.9 21.1 %reduce-scatter.5.cloned.1.call-done = bf16[1,256,128]{1,2,0:T(8,128)(2,1)} async-done(((bf16[1,1024,128]{1,2,0:T(8,128)(2,1)}), bf16[1,256,128]{1,2,0:T(8,128)(2,1)}) %reduce-scatter.5.cloned.1.call-update) | async-done | bytes 65552 | tf_op jit(solution)/shard_map/while/body/eval_jaxpr/reduce_scatter | solution.py:275
  697.4 3.6 fusion.229
  701.0 2.6 convolution_convert_fusion.11
  703.7 3.5 fusion.228
  708.8 12.4 %reduce-scatter.3.cloned.1.call-done = bf16[1,256,128]{1,2,0:T(8,128)(2,1)} async-done(((bf16[1,1024,128]{1,2,0:T(8,128)(2,1)}), bf16[1,256,128]{1,2,0:T(8,128)(2,1)}) %reduce-scatter.3.cloned.1.call-update) | async-done | bytes 65552 | tf_op jit(solution)/shard_map/while/body/eval_jaxpr/reduce_scatter | solution.py:269
  722.7 21.0 %reduce-scatter.5.cloned.1.call-done = bf16[1,256,128]{1,2,0:T(8,128)(2,1)} async-done(((bf16[1,1024,128]{1,2,0:T(8,128)(2,1)}), bf16[1,256,128]{1,2,0:T(8,128)(2,1)}) %reduce-scatter.5.cloned.1.call-update) | async-done | bytes 65552 | tf_op jit(solution)/shard_map/while/body/eval_jaxpr/reduce_scatter | solution.py:275
  756.1 3.6 fusion.229
  759.7 2.6 convolution_convert_fusion.11
  762.3 3.5 fusion.228
  767.4 12.4 %reduce-scatter.3.cloned.1.call-done = bf16[1,256,128]{1,2,0:T(8,128)(2,1)} async-done(((bf16[1,1024,128]{1,2,0:T(8,128)(2,1)}), bf16[1,256,128]{1,2,0:T(8,128)(2,1)}) %reduce-scatter.3.cloned.1.call-update) | async-done | bytes 65552 | tf_op jit(solution)/shard_map/while/body/eval_jaxpr/reduce_scatter | solution.py:269
  781.4 21.0 %reduce-scatter.5.cloned.1.call-done = bf16[1,256,128]{1,2,0:T(8,128)(2,1)} async-done(((bf16[1,1024,128]{1,2,0:T(8,128)(2,1)}), bf16[1,256,128]{1,2,0:T(8,128)(2,1)}) %reduce-scatter.5.cloned.1.call-update) | async-done | bytes 65552 | tf_op jit(solution)/shard_map/while/body/eval_jaxpr/reduce_scatter | solution.py:275
  814.8 3.6 fusion.229
  818.4 2.6 convolution_convert_fusion.11
  821.1 3.5 fusion.228
  826.2 12.4 %reduce-scatter.3.cloned.1.call-done = bf16[1,256,128]{1,2,0:T(8,128)(2,1)} async-done(((bf16[1,1024,128]{1,2,0:T(8,128)(2,1)}), bf16[1,256,128]{1,2,0:T(8,128)(2,1)}) %reduce-scatter.3.cloned.1.call-update) | async-done | bytes 65552 | tf_op jit(solution)/shard_map/while/body/eval_jaxpr/reduce_scatter | solution.py:269
  840.1 21.2 %reduce-scatter.5.cloned.1.call-done = bf16[1,256,128]{1,2,0:T(8,128)(2,1)} async-done(((bf16[1,1024,128]{1,2,0:T(8,128)(2,1)}), bf16[1,256,128]{1,2,0:T(8,128)(2,1)}) %reduce-scatter.5.cloned.1.call-update) | async-done | bytes 65552 | tf_op jit(solution)/shard_map/while/body/eval_jaxpr/reduce_scatter | solution.py:275
  873.6 3.6 fusion.229
  877.2 2.6 convolution_convert_fusion.11
  879.8 3.5 fusion.228
  884.9 12.4 %reduce-scatter.3.cloned.1.call-done = bf16[1,256,128]{1,2,0:T(8,128)(2,1)} async-done(((bf16[1,1024,128]{1,2,0:T(8,128)(2,1)}), bf16[1,256,128]{1,2,0:T(8,128)(2,1)}) %reduce-scatter.3.cloned.1.call-update) | async-done | bytes 65552 | tf_op jit(solution)/shard_map/while/body/eval_jaxpr/reduce_scatter | solution.py:269
  898.9 21.2 %reduce-scatter.5.cloned.1.call-done = bf16[1,256,128]{1,2,0:T(8,128)(2,1)} async-done(((bf16[1,1024,128]{1,2,0:T(8,128)(2,1)}), bf16[1,256,128]{1,2,0:T(8,128)(2,1)}) %reduce-scatter.5.cloned.1.call-update) | async-done | bytes 65552 | tf_op jit(solution)/shard_map/while/body/eval_jaxpr/reduce_scatter | solution.py:275
  932.4 3.6 fusion.229
  938.7 3.5 fusion.228
  943.8 12.4 %reduce-scatter.3.cloned.1.call-done = bf16[1,256,128]{1,2,0:T(8,128)(2,1)} async-done(((bf16[1,1024,128]{1,2,0:T(8,128)(2,1)}), bf16[1,256,128]{1,2,0:T(8,128)(2,1)}) %reduce-scatter.3.cloned.1.call-update) | async-done | bytes 65552 | tf_op jit(solution)/shard_map/while/body/eval_jaxpr/reduce_scatter | solution.py:269
  957.7 21.2 %reduce-scatter.5.cloned.1.call-done = bf16[1,256,128]{1,2,0:T(8,128)(2,1)} async-done(((bf16[1,1024,128]{1,2,0:T(8,128)(2,1)}), bf16[1,256,128]{1,2,0:T(8,128)(2,1)}) %reduce-scatter.5.cloned.1.call-update) | async-done | bytes 65552 | tf_op jit(solution)/shard_map/while/body/eval_jaxpr/reduce_scatter | solution.py:275
  994.1 5.0 fusion.107
  1000.0 4.7 fusion.120
  1007.6 166.9 %all-reduce.7.cloned.1.call-done = (f32[8,16,1024]{2,1,0:T(8,128)}, f32[8,16,3072]{2,1,0:T(8,128)}, f32[8,16,1024]{2,1,0:T(8,128)}, f32[8,16,1024]{2,1,0:T(8,128...) async-done(((f32[8,16,1024]{2,1,0:T(8,128)}, f32[8,16,3072]{2,1,0:T(8,128)}, f32[8,16,1024]{2,1,0:T(8,128)}, ...) | async-done | bytes 8224784 | tf_op jit(solution)/shard_map/psum | solution.py:304
  1176.4 2.9 copy.196
  (477 shorter events, 230.4 us)
Async XLA Ops:
  7.2 161.9 %copy-start = (bf16[8,16,5248]{2,1,0:T(8,128)(2,1)S(1)}, bf16[8,16,5248]{2,1,0:T(8,128)(2,1)}, u32[]{:S(2)}) copy-start(bf16[8,16,5248]{2,1,0:T(8,128)(2,1)} %param.37) | copy-start | bytes 4030468
  7.2 21.5 %copy-start.54 = (bf16[256]{0:T(256)(128)(2,1)S(1)}, bf16[256]{0:T(256)(128)(2,1)}, u32[]{:S(2)}) copy-start(bf16[256]{0:T(256)(128)(2,1)} %param.30) | copy-start | bytes 1540
  7.2 112.3 %all-gather.10.cloned.1.call-start = ((), (), s32[]{:S(2)}) async-start(), calls=%async_computation.2 | async-start | bytes 7077888 | tf_op jit(solution)/shard_map/all_gather | solution.py:150
  19.1 136.7 %all-gather.18.cloned.1.call-start = ((), (), s32[]{:S(2)}) async-start(), calls=%async_computation.6 | async-start | bytes 1679360 | tf_op jit(solution)/shard_map/all_gather | solution.py:144
  19.8 208.9 %all-gather.22.cloned.1.call-start = ((), (), s32[]{:S(2)}) async-start(), calls=%async_computation.8 | async-start | bytes 6045696 | tf_op jit(solution)/shard_map/all_gather | solution.py:153
  28.6 222.9 %all-gather.14.cloned.1.call-start = ((), (), s32[]{:S(2)}) async-start(), calls=%async_computation.4 | async-start | bytes 2621440 | tf_op jit(solution)/shard_map/all_gather | solution.py:174
  34.8 6.3 copy-start.29
  35.9 5.2 copy-start.3
  35.9 5.7 copy-start.49
  42.5 81.6 %copy-start.18 = (bf16[256,1024]{1,0:T(8,128)(2,1)}, bf16[256,1024]{1,0:T(8,128)(2,1)S(1)}, u32[]{:S(2)}) copy-start(bf16[256,1024]{1,0:T(8,128)(2,1)S(1)} %fusion.67) | copy-start | bytes 1572868
  119.5 4.6 copy-start.38
  142.6 6.7 copy-start.53
  146.9 9.7 copy-start.55
  146.9 15.2 %copy-start.40 = (s32[1,1024]{1,0:T(1,128)S(1)}, s32[1,1024]{1,0:T(1,128)}, u32[]{:S(2)}) copy-start(s32[1,1024]{1,0:T(1,128)} %param.24) | copy-start | bytes 12292
  146.9 15.2 %copy-start.50 = (bf16[8,16,1024]{2,1,0:T(8,128)(2,1)S(1)}, bf16[8,16,1024]{2,1,0:T(8,128)(2,1)}, u32[]{:S(2)}) copy-start(bf16[8,16,1024]{2,1,0:T(8,128)(2,1)} %param.34) | copy-start | bytes 786436
  146.9 129.2 %all-gather.12.cloned.1.call-start = ((), (), s32[]{:S(2)}) async-start(), calls=%async_computation.3 | async-start | bytes 2621440 | tf_op jit(solution)/shard_map/all_gather | solution.py:175
  149.2 18.1 %copy-start.13 = (bf16[1,256,1024]{2,1,0:T(8,128)(2,1)S(1)}, bf16[1,256,1024]{2,1,0:T(8,128)(2,1)}, u32[]{:S(2)}) copy-start(bf16[1,256,1024]{2,1,0:T(8,128)(2,1)} %param.23) | copy-start | bytes 1572868
  149.3 179.9 %all-gather.16.cloned.1.call-start = ((), (), s32[]{:S(2)}) async-start(), calls=%async_computation.5 | async-start | bytes 2359296 | tf_op jit(solution)/shard_map/all_gather | solution.py:151
  155.7 327.9 %all-gather.20.cloned.1.call-start = ((), (), s32[]{:S(2)}) async-start(), calls=%async_computation.7 | async-start | bytes 12091392 | tf_op jit(solution)/shard_map/all_gather | solution.py:152
  156.6 13.0 %copy-start.10 = (bf16[8,1,256,128]{2,3,1,0:T(8,128)(2,1)}, bf16[8,1,256,128]{2,3,1,0:T(8,128)(2,1)S(1)}, u32[]{:S(2)}) copy-start(bf16[8,1,256,128]{2,3,1,0:T(8,128)(2,1)S(1)} %fusion.114) | copy-start | bytes 1572868
  169.1 63.9 %copy-start.27 = (bf16[1,16,2624]{2,0,1:T(2,128)(2,1)}, bf16[1,16,2624]{2,0,1:T(2,128)(2,1)S(1)}, u32[]{:S(2)}) copy-start(bf16[1,16,2624]{2,0,1:T(2,128)(2,1)S(1)} %fusion.62) | copy-start | bytes 251908
  255.5 24.6 %copy-start.12 = (bf16[8,1,256,128]{2,3,1,0:T(8,128)(2,1)S(1)}, bf16[8,1,256,128]{2,3,1,0:T(8,128)(2,1)}, u32[]{:S(2)}) copy-start(bf16[8,1,256,128]{2,3,1,0:T(8,128)(2,1)} %copy-done.10) | copy-start | bytes 1572868
  280.1 45.8 %copy-start.48 = (bf16[1,16,1024]{2,0,1:T(2,128)(2,1)S(1)}, bf16[1,16,1024]{2,0,1:T(2,128)(2,1)}, u32[]{:S(2)}) copy-start(bf16[1,16,1024]{2,0,1:T(2,128)(2,1)} %fusion.79) | copy-start | bytes 98308
  498.1 4.7 slice-start
  498.1 4.7 slice-start.1
  500.0 3.0 slice-start.2
  506.9 3.1 copy-start.9
  511.9 32.9 %reduce-scatter.3.cloned.1.call-start = ((), (), s32[]{:S(2)}) async-start(), calls=%async_computation.10 | async-start | bytes 327680 | tf_op jit(solution)/shard_map/while/body/eval_jaxpr/reduce_scatter | solution.py:269
  522.8 6.3 copy-start.17
  526.4 41.0 %reduce-scatter.5.cloned.1.call-start = ((), (), s32[]{:S(2)}) async-start(), calls=%async_computation.11 | async-start | bytes 327680 | tf_op jit(solution)/shard_map/while/body/eval_jaxpr/reduce_scatter | solution.py:275
  568.9 34.7 %reduce-scatter.3.cloned.1.call-start = ((), (), s32[]{:S(2)}) async-start(), calls=%async_computation.10 | async-start | bytes 327680 | tf_op jit(solution)/shard_map/while/body/eval_jaxpr/reduce_scatter | solution.py:269
  579.8 6.3 copy-start.17
  583.4 42.8 %reduce-scatter.5.cloned.1.call-start = ((), (), s32[]{:S(2)}) async-start(), calls=%async_computation.11 | async-start | bytes 327680 | tf_op jit(solution)/shard_map/while/body/eval_jaxpr/reduce_scatter | solution.py:275
  627.7 34.7 %reduce-scatter.3.cloned.1.call-start = ((), (), s32[]{:S(2)}) async-start(), calls=%async_computation.10 | async-start | bytes 327680 | tf_op jit(solution)/shard_map/while/body/eval_jaxpr/reduce_scatter | solution.py:269
  638.6 6.3 copy-start.17
  642.2 42.8 %reduce-scatter.5.cloned.1.call-start = ((), (), s32[]{:S(2)}) async-start(), calls=%async_computation.11 | async-start | bytes 327680 | tf_op jit(solution)/shard_map/while/body/eval_jaxpr/reduce_scatter | solution.py:275
  686.5 34.7 %reduce-scatter.3.cloned.1.call-start = ((), (), s32[]{:S(2)}) async-start(), calls=%async_computation.10 | async-start | bytes 327680 | tf_op jit(solution)/shard_map/while/body/eval_jaxpr/reduce_scatter | solution.py:269
  697.4 6.3 copy-start.17
  701.0 42.7 %reduce-scatter.5.cloned.1.call-start = ((), (), s32[]{:S(2)}) async-start(), calls=%async_computation.11 | async-start | bytes 327680 | tf_op jit(solution)/shard_map/while/body/eval_jaxpr/reduce_scatter | solution.py:275
  745.2 34.7 %reduce-scatter.3.cloned.1.call-start = ((), (), s32[]{:S(2)}) async-start(), calls=%async_computation.10 | async-start | bytes 327680 | tf_op jit(solution)/shard_map/while/body/eval_jaxpr/reduce_scatter | solution.py:269
  756.0 6.3 copy-start.17
  759.6 42.8 %reduce-scatter.5.cloned.1.call-start = ((), (), s32[]{:S(2)}) async-start(), calls=%async_computation.11 | async-start | bytes 327680 | tf_op jit(solution)/shard_map/while/body/eval_jaxpr/reduce_scatter | solution.py:275
  803.9 34.7 %reduce-scatter.3.cloned.1.call-start = ((), (), s32[]{:S(2)}) async-start(), calls=%async_computation.10 | async-start | bytes 327680 | tf_op jit(solution)/shard_map/while/body/eval_jaxpr/reduce_scatter | solution.py:269
  814.8 6.3 copy-start.17
  818.4 42.9 %reduce-scatter.5.cloned.1.call-start = ((), (), s32[]{:S(2)}) async-start(), calls=%async_computation.11 | async-start | bytes 327680 | tf_op jit(solution)/shard_map/while/body/eval_jaxpr/reduce_scatter | solution.py:275
  862.7 34.6 %reduce-scatter.3.cloned.1.call-start = ((), (), s32[]{:S(2)}) async-start(), calls=%async_computation.10 | async-start | bytes 327680 | tf_op jit(solution)/shard_map/while/body/eval_jaxpr/reduce_scatter | solution.py:269
  873.6 6.3 copy-start.17
  877.2 42.9 %reduce-scatter.5.cloned.1.call-start = ((), (), s32[]{:S(2)}) async-start(), calls=%async_computation.11 | async-start | bytes 327680 | tf_op jit(solution)/shard_map/while/body/eval_jaxpr/reduce_scatter | solution.py:275
  921.5 34.7 %reduce-scatter.3.cloned.1.call-start = ((), (), s32[]{:S(2)}) async-start(), calls=%async_computation.10 | async-start | bytes 327680 | tf_op jit(solution)/shard_map/while/body/eval_jaxpr/reduce_scatter | solution.py:269
  932.4 6.3 copy-start.17
  936.0 42.9 %reduce-scatter.5.cloned.1.call-start = ((), (), s32[]{:S(2)}) async-start(), calls=%async_computation.11 | async-start | bytes 327680 | tf_op jit(solution)/shard_map/while/body/eval_jaxpr/reduce_scatter | solution.py:275
  980.4 194.1 %all-reduce.7.cloned.1.call-start = ((), (), s32[]{:S(2)}) async-start(), calls=%async_computation.9 | async-start | bytes 16515072 | tf_op jit(solution)/shard_map/psum | solution.py:304
  987.7 3.1 copy-start.19
  987.7 3.3 copy-start.14
  989.5 3.0 copy-start.46
  989.5 3.0 copy-start.47
  994.1 5.0 copy-start.4
  994.1 5.0 copy-start.43
  1000.0 4.7 copy-start.52
  1174.5 4.8 copy-start.35
  1174.5 5.6 copy-start.34
  1176.4 4.5 copy-start.33
  1176.4 5.2 copy-start.22
  1181.7 4.5 copy-start.1
  (40 other events, 59.8 us)
Sparse Core Ops, SparseCore 0:
  19.2 100.2 all-gather.9
  121.1 16.6 all-gather.17
  139.8 88.8 all-gather.21
  230.7 20.7 all-gather.13
  253.5 22.5 all-gather.11
  278.0 51.1 all-gather.15
  331.4 152.2 all-gather.19
  526.5 18.2 reduce-scatter.2
  547.4 19.9 reduce-scatter.4
  583.5 20.0 reduce-scatter.2
  606.2 19.9 reduce-scatter.4
  642.3 20.0 reduce-scatter.2
  665.0 19.9 reduce-scatter.4
  701.1 20.0 reduce-scatter.2
  723.7 20.0 reduce-scatter.4
  759.8 20.0 reduce-scatter.2
  782.3 20.0 reduce-scatter.4
  818.5 20.0 reduce-scatter.2
  841.2 20.0 reduce-scatter.4
  877.3 20.0 reduce-scatter.2
  900.0 20.0 reduce-scatter.4
  936.1 20.0 reduce-scatter.2
  958.8 20.0 reduce-scatter.4
  994.2 180.2 all-reduce.6
where the time goes:
time: 1200 us; the launch traced here: 1190 us
  waiting for transfers between devices  760 us (63%)
  matrix products  161 us (13%)
  local copies, waits for them, and re-layouts  125 us (10%)
  other arithmetic  65.6 us (5%)
  blocking collectives  37.7 us (3%)
  loops' own time  27.1 us (2%)
  between operations  15.8 us (1%)
    reduce_scatter x8, waiting for transfers between devices, summed_group(): lax.psum_scatter(grad_value.reshape(seq_count, seq_length, group_width).a...  169 us
    psum x1, waiting for transfers between devices, body(): lax.psum((spread_back(terms[0], onehot), spread_back(terms[1], onehot), s...  167 us
    all_gather x1, waiting for transfers between devices, body(): lax.all_gather(tok_parts[2], 'seq', axis=1, tiled=True)  151 us
    reduce_scatter x8, waiting for transfers between devices, summed_group(): lax.psum_scatter(grad_key.reshape(seq_count, seq_length, group_width).ast...  97.5 us
    all_gather x1, waiting for transfers between devices, body(): lax.all_gather(tok_parts[0], 'seq', axis=1, tiled=True)  75.4 us
    all_gather x1, waiting for transfers between devices, body(): lax.all_gather(tok_parts[3], 'seq', axis=1, tiled=True)  59.1 us
    dynamic_slice x48, local copies, waits for them, and re-layouts, heads_slice(): lax.dynamic_slice_in_dim(source, group_index * group_width, group_width, 2)  48.9 us
    dot_general x8, matrix products, summed_group(): jnp.einsum('shqk,sqhd->skhd', grad_scores, query_part, preferred_element_...  28.5 us
  transfers between devices with their start and end apart: 24, of which 23 were waited for; matrix products, arithmetic and copies ran while one was open for 16% of the time, Pallas kernels for 0%

commit v1 on v0

--- a/solution.py
+++ b/solution.py
@@ -146,10 +146,42 @@
         lax.all_gather(attn_gain, "tok", axis=0, tiled=True),
         lax.all_gather(mlp_gain, "tok", axis=0, tiled=True),
     )
+
+    def track_matrix(on_dim, work_x):
+        lane_axis = "seq"
+        v1, placed, right_arr = (
+            lax.axis_size(lane_axis),
+            lax.axis_index(lane_axis),
+            work_x.shape[on_dim],
+        )
+        z_new = lax.dynamic_update_slice_in_dim(
+            jnp.zeros(
+                [nth * v1 if i0 == on_dim else nth for i0, nth in enumerate(work_x.shape)],
+                work_x.dtype,
+            ),
+            work_x,
+            placed * right_arr,
+            axis=on_dim,
+        )
+        seen_now = even = work_x
+        no = 1
+        while no < v1 // 2 + 1:
+            seen_now = lax.ppermute(seen_now, lane_axis, [(i0, (i0 + 1) % v1) for i0 in range(v1)])
+            z_new = lax.dynamic_update_slice_in_dim(
+                z_new, seen_now, (placed - no) % v1 * right_arr, axis=on_dim
+            )
+            if 2 * no < v1:
+                even = lax.ppermute(even, lane_axis, [(i0, (i0 - 1) % v1) for i0 in range(v1)])
+                z_new = lax.dynamic_update_slice_in_dim(
+                    z_new, even, (placed + no) % v1 * right_arr, axis=on_dim
+                )
+            no = no + 1
+        return z_new
+
     w_qkv, w_out, w_in, w_out2 = (
         lax.all_gather(tok_parts[0], "seq", axis=1, tiled=True),
         lax.all_gather(tok_parts[1], "seq", axis=1, tiled=True),
-        lax.all_gather(tok_parts[2], "seq", axis=1, tiled=True),
+        track_matrix(1, tok_parts[2]),
         lax.all_gather(tok_parts[3], "seq", axis=1, tiled=True),
     )
     gain_one = tok_parts[4].astype(jnp.float32)

time: 1200 us -> 1290 us (1.075)
  waiting for transfers between devices: 760 us -> 796 us
  local copies, waits for them, and re-layouts: 125 us -> 149 us
  starting transfers between devices: 0.87 us -> 16.6 us
    ppermute x0 -> x7, waiting for transfers between devices: none -> 183 us  [the longest x4 180 us: track_matrix(): lax.ppermute(seen_now, lane_axis, [(i0, (i0 + 1) % v1) for i0 in range(v1)])]
    all_gather x1, waiting for transfers between devices: 59.1 us -> 0.01 us  [body(): lax.all_gather(tok_parts[3], 'seq', axis=1, tiled=True)]
    all_gather x1, waiting for transfers between devices: 151 us -> 99 us  [body(): lax.all_gather(back_parts[2], 'seq', axis=1, tiled=True)]
    all_gather x1, waiting for transfers between devices: 20.6 us -> 0.01 us  [body(): lax.all_gather(value_low, 'tok', axis=1, tiled=True)]
    dynamic_update_slice x0 -> x8, local copies, waits for them, and re-layouts: none -> 18.8 us  [the longest x4 10.1 us: track_matrix(): lax.dynamic_update_slice_in_dim(z_new, seen_now, (placed - no) % v1 * rig...]
    ppermute x0 -> x7, starting transfers between devices: none -> 16 us  [the longest x4 8.97 us: track_matrix(): lax.ppermute(seen_now, lane_axis, [(i0, (i0 + 1) % v1) for i0 in range(v1)])]
    all_gather x1, waiting for transfers between devices: 15.5 us -> 0.01 us  [body(): lax.all_gather(key_low, 'tok', axis=1, tiled=True)]
    unnamed x125 -> x127, local copies, waits for them, and re-layouts: 28.1 us -> 25.8 us
  transfers between devices with their start and end apart: 24 -> 31, of which waited for: 23 -> 23; matrix products, arithmetic and copies ran while one was open for 16% -> 18% of each run, Pallas kernels for 0% -> 0%
where the time goes in v1:
time: 1290 us; the launch traced here: 1280 us
  waiting for transfers between devices  796 us (62%)
  matrix products  165 us (13%)
  local copies, waits for them, and re-layouts  149 us (12%)
  other arithmetic  64.4 us (5%)
  blocking collectives  47.9 us (4%)
  loops' own time  27.1 us (2%)
  starting transfers between devices  16.6 us (1%)
  between operations  15.9 us (1%)
    ppermute x4, waiting for transfers between devices, track_matrix(): lax.ppermute(seen_now, lane_axis, [(i0, (i0 + 1) % v1) for i0 in range(v1)])  180 us
    reduce_scatter x8, waiting for transfers between devices, summed_group(): lax.psum_scatter(grad_value.reshape(seq_count, seq_length, group_width).a...  174 us
    psum x1, waiting for transfers between devices, body(): lax.psum((spread_back(terms[0], onehot), spread_back(terms[1], onehot), s...  166 us
    all_gather x1, waiting for transfers between devices, body(): lax.all_gather(back_parts[2], 'seq', axis=1, tiled=True)  99 us
    reduce_scatter x8, waiting for transfers between devices, summed_group(): lax.psum_scatter(grad_key.reshape(seq_count, seq_length, group_width).ast...  97.3 us
    all_gather x1, waiting for transfers between devices, body(): lax.all_gather(tok_parts[0], 'seq', axis=1, tiled=True)  75.4 us
    dynamic_slice x48, local copies, waits for them, and re-layouts, heads_slice(): lax.dynamic_slice_in_dim(source, group_index * group_width, group_width, 2)  49.1 us
    dot_general x8, matrix products, summed_group(): jnp.einsum('shqk,sqhd->skhd', grad_scores, query_part, preferred_element_...  28.5 us
  transfers between devices with their start and end apart: 31, of which 23 were waited for; matrix products, arithmetic and copies ran while one was open for 18% of the time, Pallas kernels for 0%

profile of v1, /device:TPU:0, one launch (start us, length us, event | category | flops | bytes accessed | tf_op | source)
XLA Modules:
  0.0 1281.5 jit_solution(13585343045302111767)
XLA Ops:
  7.3 11.8 all_gather.44
  19.9 8.8 all_gather.52
  28.7 5.2 all-gather
  44.1 75.4 %all-gather.10.cloned.1.call-done = bf16[1024,3072]{1,0:T(8,128)(2,1)} async-done(((bf16[1024,384]{1,0:T(8,128)(2,1)}), bf16[1024,3072]{1,0:T(8,128)(2,1)}) %all-gather.10.cloned.1.call-update) | async-done | bytes 6291472 | tf_op jit(solution)/shard_map/all_gather | solution.py:182
  119.5 4.6 fusion.118
  126.4 3.2 fusion.112
  144.4 4.3 add_convert_fusion.4
  152.6 6.2 all_gather.48
  158.9 3.3 collective-permute-start.1
  162.2 53.6 %collective-permute-done = bf16[1024,656]{0,1:T(8,128)(2,1)} collective-permute-done((bf16[1024,656]{0,1:T(8,128)(2,1)}, bf16[1024,656]{0,1:T(8,128)(2,1)}, u32[]{:S(2)}, u32[]{:S(2)}) %collective-permute-start) | collective-permute-done | bytes 1343520 | tf_op jit(solution)/shard_map/ppermute | solution.py:169
  222.3 77.5 %collective-permute-done.2 = bf16[1024,656]{0,1:T(8,128)(2,1)} collective-permute-done((bf16[1024,656]{0,1:T(8,128)(2,1)}, bf16[1024,656]{0,1:T(8,128)(2,1)}, u32[]{:S(2)}, u32[]{:S(2)}) %collective-permute-start.2) | collective-permute-done | bytes 1343520 | tf_op jit(solution)/shard_map/ppermute | solution.py:169
  307.4 3.1 collective-permute-start.5
  310.5 49.4 %collective-permute-done.4 = bf16[1024,656]{0,1:T(8,128)(2,1)} collective-permute-done((bf16[1024,656]{0,1:T(8,128)(2,1)}, bf16[1024,656]{0,1:T(8,128)(2,1)}, u32[]{:S(2)}, u32[]{:S(2)}) %collective-permute-start.4) | collective-permute-done | bytes 1343520 | tf_op jit(solution)/shard_map/ppermute | solution.py:169
  362.4 16.0 %all-gather.1 = bf16[4,1,256]{2,1,0:T(2,128)(2,1)S(1)} all-gather(bf16[1,1,256]{2,1,0:T(2,128)(2,1)S(1)} %reshape.799), channel_id=1, replica_groups=mesh['seq'=8,'tok'=4] {'tok'}, dimensions={0}, use_global_device_ids=true | all-gather | bytes 2560 | tf_op jit(solution)/shard_map/all_gather | solution.py:147
  378.9 5.3 broadcast_in_dim.97
  403.0 4.2 fusion.71
  410.4 4.0 copy.83
  414.3 4.0 copy.81
  418.4 45.8 %while.30 = (s32[]{:T(128)}, bf16[8,1,256,128]{2,3,1,0:T(8,128)(2,1)S(1)}, f32[8,1,2,256]{3,2,1,0:T(2,128)}, s32[8]{0:T(128)S(1)}, bf16[1,1024,1024]{1,2,0:T(8,1...) while((s32[]{:T(128)}, ...), condition=%wide.region_5.6_spmd.clone.clone, body=%wide.region_2.5_spmd.clone.sunk.clone | while | flops 138149376 | bytes 8804011 | solution.py:224
  468.9 6.0 fusion.26
  474.8 6.5 fusion.48
  488.9 99.0 %all-gather.22.cloned.1.call-done = bf16[1024,5248]{0,1:T(8,128)(2,1)} async-done(((bf16[1024,656]{0,1:T(8,128)(2,1)}), bf16[1024,5248]{0,1:T(8,128)(2,1)}) %all-gather.22.cloned.1.call-update) | async-done | bytes 10747920 | tf_op jit(solution)/shard_map/all_gather | solution.py:242
  587.9 6.7 fusion.61
  600.6 473.0 %while.31 = (s32[]{:T(128)}, f32[8,1,256,128]{2,3,1,0:T(8,128)}, f32[8,1,256,128]{2,3,1,0:T(8,128)}, bf16[8,1,256,128]{2,3,1,0:T(8,128)(2,1)}, s32[8]{0:T(128)S(...) while((s32[]{:T(128)}, f32[8,1,256,128]{2,3,1,0:T(8,128)}, ...), condition=%wide.region_14.15_spmd.clone.clone, body=%wide.region_10.14_spmd.clone.sunk.clone | while | flops 343477248 | bytes 23342488 | solution.py:316
  611.4 3.6 fusion.229
  615.1 2.6 convolution_convert_fusion.11
  617.7 3.6 fusion.228
  622.8 10.5 reduce-scatter.3.cloned.1.call-done
  634.9 21.8 %reduce-scatter.5.cloned.1.call-done = bf16[1,256,128]{1,2,0:T(8,128)(2,1)} async-done(((bf16[1,1024,128]{1,2,0:T(8,128)(2,1)}), bf16[1,256,128]{1,2,0:T(8,128)(2,1)}) %reduce-scatter.5.cloned.1.call-update) | async-done | bytes 65552 | tf_op jit(solution)/shard_map/while/body/eval_jaxpr/reduce_scatter | solution.py:307
  669.0 3.6 fusion.229
  672.7 2.6 convolution_convert_fusion.11
  675.3 3.5 fusion.228
  680.4 12.4 reduce-scatter.3.cloned.1.call-done
  694.3 21.8 %reduce-scatter.5.cloned.1.call-done = bf16[1,256,128]{1,2,0:T(8,128)(2,1)} async-done(((bf16[1,1024,128]{1,2,0:T(8,128)(2,1)}), bf16[1,256,128]{1,2,0:T(8,128)(2,1)}) %reduce-scatter.5.cloned.1.call-update) | async-done | bytes 65552 | tf_op jit(solution)/shard_map/while/body/eval_jaxpr/reduce_scatter | solution.py:307
  728.4 3.6 fusion.229
  734.7 3.5 fusion.228
  739.8 12.4 reduce-scatter.3.cloned.1.call-done
  753.6 21.7 %reduce-scatter.5.cloned.1.call-done = bf16[1,256,128]{1,2,0:T(8,128)(2,1)} async-done(((bf16[1,1024,128]{1,2,0:T(8,128)(2,1)}), bf16[1,256,128]{1,2,0:T(8,128)(2,1)}) %reduce-scatter.5.cloned.1.call-update) | async-done | bytes 65552 | tf_op jit(solution)/shard_map/while/body/eval_jaxpr/reduce_scatter | solution.py:307
  787.8 3.6 fusion.229
  791.4 2.6 convolution_convert_fusion.11
  794.1 3.5 fusion.228
  799.2 12.4 reduce-scatter.3.cloned.1.call-done
  813.0 21.6 %reduce-scatter.5.cloned.1.call-done = bf16[1,256,128]{1,2,0:T(8,128)(2,1)} async-done(((bf16[1,1024,128]{1,2,0:T(8,128)(2,1)}), bf16[1,256,128]{1,2,0:T(8,128)(2,1)}) %reduce-scatter.5.cloned.1.call-update) | async-done | bytes 65552 | tf_op jit(solution)/shard_map/while/body/eval_jaxpr/reduce_scatter | solution.py:307
  847.1 3.6 fusion.229
  853.3 3.5 fusion.228
  858.4 12.4 reduce-scatter.3.cloned.1.call-done
  872.3 21.6 %reduce-scatter.5.cloned.1.call-done = bf16[1,256,128]{1,2,0:T(8,128)(2,1)} async-done(((bf16[1,1024,128]{1,2,0:T(8,128)(2,1)}), bf16[1,256,128]{1,2,0:T(8,128)(2,1)}) %reduce-scatter.5.cloned.1.call-update) | async-done | bytes 65552 | tf_op jit(solution)/shard_map/while/body/eval_jaxpr/reduce_scatter | solution.py:307
  906.3 3.6 fusion.229
  912.5 3.5 fusion.228
  917.6 12.4 reduce-scatter.3.cloned.1.call-done
  931.5 21.7 %reduce-scatter.5.cloned.1.call-done = bf16[1,256,128]{1,2,0:T(8,128)(2,1)} async-done(((bf16[1,1024,128]{1,2,0:T(8,128)(2,1)}), bf16[1,256,128]{1,2,0:T(8,128)(2,1)}) %reduce-scatter.5.cloned.1.call-update) | async-done | bytes 65552 | tf_op jit(solution)/shard_map/while/body/eval_jaxpr/reduce_scatter | solution.py:307
  965.7 3.6 fusion.229
  971.9 3.5 fusion.228
  977.0 12.4 reduce-scatter.3.cloned.1.call-done
  990.9 21.8 %reduce-scatter.5.cloned.1.call-done = bf16[1,256,128]{1,2,0:T(8,128)(2,1)} async-done(((bf16[1,1024,128]{1,2,0:T(8,128)(2,1)}), bf16[1,256,128]{1,2,0:T(8,128)(2,1)}) %reduce-scatter.5.cloned.1.call-update) | async-done | bytes 65552 | tf_op jit(solution)/shard_map/while/body/eval_jaxpr/reduce_scatter | solution.py:307
  1025.1 3.6 fusion.229
  1028.7 2.6 convolution_convert_fusion.11
  1031.3 3.5 fusion.228
  1036.4 12.4 reduce-scatter.3.cloned.1.call-done
  1050.4 21.7 %reduce-scatter.5.cloned.1.call-done = bf16[1,256,128]{1,2,0:T(8,128)(2,1)} async-done(((bf16[1,1024,128]{1,2,0:T(8,128)(2,1)}), bf16[1,256,128]{1,2,0:T(8,128)(2,1)}) %reduce-scatter.5.cloned.1.call-update) | async-done | bytes 65552 | tf_op jit(solution)/shard_map/while/body/eval_jaxpr/reduce_scatter | solution.py:307
  1083.4 4.3 fusion.120
  1088.9 4.8 fusion.108
  1096.4 166.1 %all-reduce.7.cloned.1.call-done = (f32[8,16,1024]{2,1,0:T(8,128)}, f32[8,16,3072]{2,1,0:T(8,128)}, f32[8,16,1024]{2,1,0:T(8,128)}, f32[8,16,1024]{2,1,0:T(8,128...) async-done(((f32[8,16,1024]{2,1,0:T(8,128)}, f32[8,16,3072]{2,1,0:T(8,128)}, f32[8,16,1024]{2,1,0:T(8,128)}, ...) | async-done | bytes 8224784 | tf_op jit(solution)/shard_map/psum | solution.py:336
  1264.5 2.9 copy.204
  (501 shorter events, 264.1 us)
Async XLA Ops:
  7.2 371.2 %copy-start = (bf16[8,16,5248]{2,1,0:T(8,128)(2,1)S(1)}, bf16[8,16,5248]{2,1,0:T(8,128)(2,1)}, u32[]{:S(2)}) copy-start(bf16[8,16,5248]{2,1,0:T(8,128)(2,1)} %param.37) | copy-start | bytes 4030468
  7.2 21.5 %copy-start.58 = (bf16[256]{0:T(256)(128)(2,1)S(1)}, bf16[256]{0:T(256)(128)(2,1)}, u32[]{:S(2)}) copy-start(bf16[256]{0:T(256)(128)(2,1)} %param.30) | copy-start | bytes 1540
  7.2 112.3 %all-gather.10.cloned.1.call-start = ((), (), s32[]{:S(2)}) async-start(), calls=%async_computation.2 | async-start | bytes 7077888 | tf_op jit(solution)/shard_map/all_gather | solution.py:182
  19.1 132.0 %all-gather.18.cloned.1.call-start = ((), (), s32[]{:S(2)}) async-start(), calls=%async_computation.6 | async-start | bytes 1679360 | tf_op jit(solution)/shard_map/all_gather | solution.py:144
  19.8 383.2 %all-gather.20.cloned.1.call-start = ((), (), s32[]{:S(2)}) async-start(), calls=%async_computation.7 | async-start | bytes 6045696 | tf_op jit(solution)/shard_map/all_gather | solution.py:185
  28.6 381.7 %all-gather.14.cloned.1.call-start = ((), (), s32[]{:S(2)}) async-start(), calls=%async_computation.4 | async-start | bytes 2621440 | tf_op jit(solution)/shard_map/all_gather | solution.py:206
  34.8 6.3 copy-start.29
  35.9 5.2 copy-start.4
  35.9 5.7 copy-start.52
  42.5 81.6 %copy-start.18 = (bf16[256,1024]{1,0:T(8,128)(2,1)}, bf16[256,1024]{1,0:T(8,128)(2,1)S(1)}, u32[]{:S(2)}) copy-start(bf16[256,1024]{1,0:T(8,128)(2,1)S(1)} %fusion.67) | copy-start | bytes 1572868
  119.5 4.6 copy-start.40
  144.4 8.2 copy-start.57
  148.7 72.7 %copy-start.53 = (bf16[8,16,1024]{2,1,0:T(8,128)(2,1)S(1)}, bf16[8,16,1024]{2,1,0:T(8,128)(2,1)}, u32[]{:S(2)}) copy-start(bf16[8,16,1024]{2,1,0:T(8,128)(2,1)} %param.34) | copy-start | bytes 786436
  148.7 153.7 %copy-start.54 = (bf16[8,16,1024]{2,1,0:T(8,128)(2,1)S(1)}, bf16[8,16,1024]{2,1,0:T(8,128)(2,1)}, u32[]{:S(2)}) copy-start(bf16[8,16,1024]{2,1,0:T(8,128)(2,1)} %param.35) | copy-start | bytes 786436
  148.7 157.0 %copy-start.13 = (bf16[1,256,1024]{2,1,0:T(8,128)(2,1)S(1)}, bf16[1,256,1024]{2,1,0:T(8,128)(2,1)}, u32[]{:S(2)}) copy-start(bf16[1,256,1024]{2,1,0:T(8,128)(2,1)} %param.23) | copy-start | bytes 1572868
  148.7 161.8 %copy-start.42 = (s32[1,1024]{1,0:T(1,128)S(1)}, s32[1,1024]{1,0:T(1,128)}, u32[]{:S(2)}) copy-start(s32[1,1024]{1,0:T(1,128)} %param.24) | copy-start | bytes 12292
  148.7 265.6 %all-gather.12.cloned.1.call-start = ((), (), s32[]{:S(2)}) async-start(), calls=%async_computation.3 | async-start | bytes 2621440 | tf_op jit(solution)/shard_map/all_gather | solution.py:207
  151.0 211.3 %copy-start.59 = (bf16[256]{0:T(256)(128)(2,1)S(1)}, bf16[256]{0:T(256)(128)(2,1)}, u32[]{:S(2)}) copy-start(bf16[256]{0:T(256)(128)(2,1)} %param.31) | copy-start | bytes 1540
  151.0 313.4 %all-gather.16.cloned.1.call-start = ((), (), s32[]{:S(2)}) async-start(), calls=%async_computation.5 | async-start | bytes 2359296 | tf_op jit(solution)/shard_map/all_gather | solution.py:183
  151.1 64.7 %collective-permute-start = (bf16[1024,656]{0,1:T(8,128)(2,1)}, bf16[1024,656]{0,1:T(8,128)(2,1)}, u32[]{:S(2)}, u32[]{:S(2)}) collective-permute-start(bf16[1024,656]{0,1:T(8,128)(2,1)} %all-gather.18.cloned.1.call-done), channel_id=1, source_target_pairs={{0,4},{4,8},{8,12},{12,16},{16,20},{20,24},{24,28},{28,0},{1,5},{5... | collective-permute-start | bytes 4030472 | tf_op jit(solution)/shard_map/ppermute | solution.py:169
  158.9 429.0 %all-gather.22.cloned.1.call-start = ((), (), s32[]{:S(2)}) async-start(), calls=%async_computation.8 | async-start | bytes 12091392 | tf_op jit(solution)/shard_map/all_gather | solution.py:242
  158.9 61.9 %collective-permute-start.1 = (bf16[1024,656]{0,1:T(8,128)(2,1)}, bf16[1024,656]{0,1:T(8,128)(2,1)}, u32[]{:S(2)}, u32[]{:S(2)}) collective-permute-start(bf16[1024,656]{0,1:T(8,128)(2,1)} %all-gather.18.cloned.1.call-done), channel_id=1, source_target_pairs={{0,28},{4,0},{8,4},{12,8},{16,12},{20,16},{24,20},{28,24},{1,29},{... | collective-permute-start | bytes 4030472 | tf_op jit(solution)/shard_map/ppermute | solution.py:174
  215.8 84.0 %collective-permute-start.2 = (bf16[1024,656]{0,1:T(8,128)(2,1)}, bf16[1024,656]{0,1:T(8,128)(2,1)}, u32[]{:S(2)}, u32[]{:S(2)}) collective-permute-start(bf16[1024,656]{0,1:T(8,128)(2,1)} %collective-permute-done), channel_id=1, source_target_pairs={{0,4},{4,8},{8,12},{12,16},{16,20},{20,24},{24,28},{28,0},{1,5},{5... | collective-permute-start | bytes 4030472 | tf_op jit(solution)/shard_map/ppermute | solution.py:169
  220.8 86.6 %collective-permute-start.3 = (bf16[1024,656]{0,1:T(8,128)(2,1)}, bf16[1024,656]{0,1:T(8,128)(2,1)}, u32[]{:S(2)}, u32[]{:S(2)}) collective-permute-start(bf16[1024,656]{0,1:T(8,128)(2,1)} %collective-permute-done.1), channel_id=1, source_target_pairs={{0,28},{4,0},{8,4},{12,8},{16,12},{20,16},{24,20},{28,24},{1,29},{... | collective-permute-start | bytes 4030472 | tf_op jit(solution)/shard_map/ppermute | solution.py:174
  299.8 60.0 %collective-permute-start.4 = (bf16[1024,656]{0,1:T(8,128)(2,1)}, bf16[1024,656]{0,1:T(8,128)(2,1)}, u32[]{:S(2)}, u32[]{:S(2)}) collective-permute-start(bf16[1024,656]{0,1:T(8,128)(2,1)} %collective-permute-done.2), channel_id=1, source_target_pairs={{0,4},{4,8},{8,12},{12,16},{16,20},{20,24},{24,28},{28,0},{1,5},{5... | collective-permute-start | bytes 4030472 | tf_op jit(solution)/shard_map/ppermute | solution.py:169
  302.4 76.5 %copy-start.10 = (bf16[8,1,256,128]{2,3,1,0:T(8,128)(2,1)}, bf16[8,1,256,128]{2,3,1,0:T(8,128)(2,1)S(1)}, u32[]{:S(2)}) copy-start(bf16[8,1,256,128]{2,3,1,0:T(8,128)(2,1)S(1)} %fusion.115) | copy-start | bytes 1572868
  305.7 72.6 %copy-start.55 = (bf16[1,16,1024]{2,0,1:T(2,128)(2,1)}, bf16[1,16,1024]{2,0,1:T(2,128)(2,1)S(1)}, u32[]{:S(2)}) copy-start(bf16[1,16,1024]{2,0,1:T(2,128)(2,1)S(1)} %fusion.73) | copy-start | bytes 98308
  307.4 90.6 %collective-permute-start.5 = (bf16[1024,656]{0,1:T(8,128)(2,1)}, bf16[1024,656]{0,1:T(8,128)(2,1)}, u32[]{:S(2)}, u32[]{:S(2)}) collective-permute-start(bf16[1024,656]{0,1:T(8,128)(2,1)} %collective-permute-done.3), channel_id=1, source_target_pairs={{0,28},{4,0},{8,4},{12,8},{16,12},{20,16},{24,20},{28,24},{1,29},{... | collective-permute-start | bytes 4030472 | tf_op jit(solution)/shard_map/ppermute | solution.py:174
  359.9 40.6 %collective-permute-start.6 = (bf16[1024,656]{0,1:T(8,128)(2,1)}, bf16[1024,656]{0,1:T(8,128)(2,1)}, u32[]{:S(2)}, u32[]{:S(2)}) collective-permute-start(bf16[1024,656]{0,1:T(8,128)(2,1)} %collective-permute-done.4), channel_id=1, source_target_pairs={{0,4},{4,8},{8,12},{12,16},{16,20},{20,24},{24,28},{28,0},{1,5},{5... | collective-permute-start | bytes 4030472 | tf_op jit(solution)/shard_map/ppermute | solution.py:169
  378.9 5.4 copy-start.17
  418.4 45.9 %copy-start.46 = (bf16[1,16,1024]{2,0,1:T(2,128)(2,1)S(1)}, bf16[1,16,1024]{2,0,1:T(2,128)(2,1)}, u32[]{:S(2)}) copy-start(bf16[1,16,1024]{2,0,1:T(2,128)(2,1)} %fusion.79) | copy-start | bytes 98308
  468.8 6.0 copy-start.6
  600.6 32.8 %reduce-scatter.3.cloned.1.call-start = ((), (), s32[]{:S(2)}) async-start(), calls=%async_computation.10 | async-start | bytes 327680 | tf_op jit(solution)/shard_map/while/body/eval_jaxpr/reduce_scatter | solution.py:301
  611.4 6.3 copy-start.16
  615.0 41.6 %reduce-scatter.5.cloned.1.call-start = ((), (), s32[]{:S(2)}) async-start(), calls=%async_computation.11 | async-start | bytes 327680 | tf_op jit(solution)/shard_map/while/body/eval_jaxpr/reduce_scatter | solution.py:307
  658.1 34.7 %reduce-scatter.3.cloned.1.call-start = ((), (), s32[]{:S(2)}) async-start(), calls=%async_computation.10 | async-start | bytes 327680 | tf_op jit(solution)/shard_map/while/body/eval_jaxpr/reduce_scatter | solution.py:301
  669.0 6.3 copy-start.16
  672.6 43.4 %reduce-scatter.5.cloned.1.call-start = ((), (), s32[]{:S(2)}) async-start(), calls=%async_computation.11 | async-start | bytes 327680 | tf_op jit(solution)/shard_map/while/body/eval_jaxpr/reduce_scatter | solution.py:307
  717.5 34.6 %reduce-scatter.3.cloned.1.call-start = ((), (), s32[]{:S(2)}) async-start(), calls=%async_computation.10 | async-start | bytes 327680 | tf_op jit(solution)/shard_map/while/body/eval_jaxpr/reduce_scatter | solution.py:301
  728.4 6.3 copy-start.16
  732.0 43.4 %reduce-scatter.5.cloned.1.call-start = ((), (), s32[]{:S(2)}) async-start(), calls=%async_computation.11 | async-start | bytes 327680 | tf_op jit(solution)/shard_map/while/body/eval_jaxpr/reduce_scatter | solution.py:307
  776.9 34.7 %reduce-scatter.3.cloned.1.call-start = ((), (), s32[]{:S(2)}) async-start(), calls=%async_computation.10 | async-start | bytes 327680 | tf_op jit(solution)/shard_map/while/body/eval_jaxpr/reduce_scatter | solution.py:301
  787.8 6.3 copy-start.16
  791.4 43.3 %reduce-scatter.5.cloned.1.call-start = ((), (), s32[]{:S(2)}) async-start(), calls=%async_computation.11 | async-start | bytes 327680 | tf_op jit(solution)/shard_map/while/body/eval_jaxpr/reduce_scatter | solution.py:307
  836.1 34.7 %reduce-scatter.3.cloned.1.call-start = ((), (), s32[]{:S(2)}) async-start(), calls=%async_computation.10 | async-start | bytes 327680 | tf_op jit(solution)/shard_map/while/body/eval_jaxpr/reduce_scatter | solution.py:301
  847.1 6.3 copy-start.16
  850.7 43.3 %reduce-scatter.5.cloned.1.call-start = ((), (), s32[]{:S(2)}) async-start(), calls=%async_computation.11 | async-start | bytes 327680 | tf_op jit(solution)/shard_map/while/body/eval_jaxpr/reduce_scatter | solution.py:307
  895.4 34.6 %reduce-scatter.3.cloned.1.call-start = ((), (), s32[]{:S(2)}) async-start(), calls=%async_computation.10 | async-start | bytes 327680 | tf_op jit(solution)/shard_map/while/body/eval_jaxpr/reduce_scatter | solution.py:301
  906.3 6.3 copy-start.16
  909.9 43.4 %reduce-scatter.5.cloned.1.call-start = ((), (), s32[]{:S(2)}) async-start(), calls=%async_computation.11 | async-start | bytes 327680 | tf_op jit(solution)/shard_map/while/body/eval_jaxpr/reduce_scatter | solution.py:307
  954.7 34.7 %reduce-scatter.3.cloned.1.call-start = ((), (), s32[]{:S(2)}) async-start(), calls=%async_computation.10 | async-start | bytes 327680 | tf_op jit(solution)/shard_map/while/body/eval_jaxpr/reduce_scatter | solution.py:301
  965.7 6.3 copy-start.16
  969.3 43.4 %reduce-scatter.5.cloned.1.call-start = ((), (), s32[]{:S(2)}) async-start(), calls=%async_computation.11 | async-start | bytes 327680 | tf_op jit(solution)/shard_map/while/body/eval_jaxpr/reduce_scatter | solution.py:307
  1014.2 34.7 %reduce-scatter.3.cloned.1.call-start = ((), (), s32[]{:S(2)}) async-start(), calls=%async_computation.10 | async-start | bytes 327680 | tf_op jit(solution)/shard_map/while/body/eval_jaxpr/reduce_scatter | solution.py:301
  1025.1 6.3 copy-start.16
  1028.7 43.4 %reduce-scatter.5.cloned.1.call-start = ((), (), s32[]{:S(2)}) async-start(), calls=%async_computation.11 | async-start | bytes 327680 | tf_op jit(solution)/shard_map/while/body/eval_jaxpr/reduce_scatter | solution.py:307
  1073.6 188.9 %all-reduce.7.cloned.1.call-start = ((), (), s32[]{:S(2)}) async-start(), calls=%async_computation.9 | async-start | bytes 16515072 | tf_op jit(solution)/shard_map/psum | solution.py:336
  1083.4 5.5 copy-start.37
  1083.4 5.5 copy-start.39
  1088.9 4.8 copy-start.5
  1088.9 4.8 copy-start.44
  1262.5 4.8 copy-start.35
  1262.5 5.6 copy-start.34
  1264.5 5.2 copy-start.22
  (48 other events, 86.2 us)
Sparse Core Ops, SparseCore 0:
  19.2 100.2 all-gather.9
  121.1 16.6 all-gather.17
  139.8 179.7 all-gather.19
  321.7 26.6 all-gather.13
  350.4 22.5 all-gather.11
  374.9 58.5 all-gather.15
  435.6 152.2 all-gather.21
  615.1 18.1 reduce-scatter.2
  636.6 20.0 reduce-scatter.4
  672.7 19.9 reduce-scatter.2
  696.0 20.0 reduce-scatter.4
  732.1 20.0 reduce-scatter.2
  755.3 20.0 reduce-scatter.4
  791.5 19.9 reduce-scatter.2
  814.6 20.0 reduce-scatter.4
  850.8 19.9 reduce-scatter.2
  873.8 20.0 reduce-scatter.4
  910.0 19.9 reduce-scatter.2
  933.2 20.0 reduce-scatter.4
  969.4 19.9 reduce-scatter.2
  992.6 20.0 reduce-scatter.4
  1028.8 20.0 reduce-scatter.2
  1052.0 20.0 reduce-scatter.4
  1082.2 180.2 all-reduce.6
